TPU v7x, 32 devices: a whole 2x2x4 slice. The times are simulated.
32 devices in a mesh: gx: 2 (over x), gy: 4 (over z), gz: 4 (over y, core).
Axes of the slice: x: 2, y: 2, z: 4, core: 2. Of those that a mesh axis runs over, the one named last changes fastest.
Arguments:
- features: bfloat16 [2, 4, 4, 768, 256], P('gx', 'gy', 'gz'), may hold values from -6 to 6
- weight: bfloat16 [27, 256, 256], replicated, may hold values from -0.078125 to 0.078125
- upstream: bfloat16 [2, 4, 4, 768, 256], P('gx', 'gy', 'gz'), may hold values from -6 to 6
- send_rows: int32 [2, 4, 4, 6, 96], P('gx', 'gy', 'gz'), may hold values from 0 to 767
- in_rows: int32 [2, 4, 4, 27, 768], P('gx', 'gy', 'gz'), may hold values from 0 to 1343, as said below
- out_rows: int32 [2, 4, 4, 27, 768], P('gx', 'gy', 'gz'), may hold values from 0 to 767, each once within a row
- tap_pair_exists: int32 [2, 4, 4, 27, 768], P('gx', 'gy', 'gz'), may hold values from 0 to 1, as said below
Outputs:
- activated: bfloat16 [2, 4, 4, 768, 256], P('gx', 'gy', 'gz')
- grad_features: bfloat16 [2, 4, 4, 768, 256], P('gx', 'gy', 'gz')
- grad_weight: bfloat16 [27, 256, 256], replicated
Inputs may be any that keep to these rules, and one draw needn't show every extreme that they name: `in_rows`: rows below 768 are a device's own; row 768 + d * 96 + f is row f of face d of the extended rows. For each device and tap the 768 rows are distinct. `out_rows`: for each device and tap, every row appears exactly once. `tap_pair_exists`: the share of existing pairs differs from device to device and from tap to tap.
All inputs are finite; a program needn't handle non-finite values.
Results may differ from a plain program's by a relative error of at most 0.0053.
Values may be sent and summed in bfloat16 or wider, within the bound.
No kernel may reach another device: no remote copies, remote signals or barrier semaphores. Data moves between devices by JAX's collectives and lax.ppermute only.
A program may use at most 128 MiB of HBM per device.

v0:
```python
import jax
import jax.numpy as jnp
from jax import lax
from jax.sharding import PartitionSpec as P


def extended(cells, sides, width):
    for axis, dim in sides:
        count = lax.axis_size(axis)
        ends = count - 1
        head = lax.slice_in_dim(cells, 0, width, axis=dim)
        tail = lax.slice_in_dim(cells, cells.shape[dim] - width, cells.shape[dim], axis=dim)
        cells = jnp.concatenate(
            [
                lax.ppermute(tail, axis, [(i, (i + 1) % count) for i in range(ends)]),
                cells,
                lax.ppermute(head, axis, [((i + 1) % count, i) for i in range(ends)]),
            ],
            axis=dim,
        )
    return cells


def trade(stacked):
    along_x = extended(stacked[0:2], (("gx", 0),), 1)
    along_y = extended(stacked[2:4], (("gy", 0),), 1)
    along_z = extended(stacked[4:6], (("gz", 0),), 1)
    return jnp.stack([along_x[0], along_x[3], along_y[0], along_y[3], along_z[0], along_z[3]])


def pairing_tables(source_voxels, target_voxels, occupancy_flags, extended_rows):
    tap_count, own_rows = source_voxels.shape
    tap_index = jnp.arange(tap_count, dtype=jnp.int32)[:, None]
    pair_index = jnp.broadcast_to(
        jnp.arange(own_rows, dtype=jnp.int32)[None, :], (tap_count, own_rows)
    )
    inverse_out = (
        jnp.zeros((tap_count, own_rows), jnp.int32).at[tap_index, target_voxels].set(pair_index)
    )
    live_at_out = jnp.take_along_axis(occupancy_flags, inverse_out, axis=1)
    source_at_out = jnp.take_along_axis(source_voxels, inverse_out, axis=1)
    forward_source = jnp.where(live_at_out > 0, source_at_out, extended_rows)
    live_target = jnp.where(occupancy_flags > 0, target_voxels, own_rows)
    backward_target = (
        jnp.full((tap_count, extended_rows), own_rows, jnp.int32)
        .at[tap_index, source_voxels]
        .set(live_target)
    )
    return (forward_source, backward_target)


def convolution_forward_step(padded_zero, forward_source, weight, group_length):
    tap_count, own_rows = forward_source.shape
    channels = weight.shape[2]
    source_by_row = forward_source.T

    def advance(group_index, running):
        leading_tap = group_index * group_length
        picks = lax.dynamic_slice_in_dim(source_by_row, leading_tap, group_length, 1)
        kernels = lax.dynamic_slice_in_dim(weight, leading_tap, group_length, 0).reshape(
            group_length * channels, channels
        )

        def accumulate(current):
            gathered = padded_zero[picks].reshape(own_rows, group_length * channels)
            return current + jnp.dot(gathered, kernels, preferred_element_type=jnp.float32)

        return accumulate(running)

    start = jnp.zeros((own_rows, channels), jnp.float32)
    return lax.fori_loop(0, tap_count // group_length, advance, start)


def convolution_backward_step(
    padded_features, backward_target, weight, gradient_zero, group_length
):
    tap_count, extended_rows = backward_target.shape
    channels = weight.shape[2]
    target_by_row = backward_target.T
    flipped = jnp.transpose(weight, (0, 2, 1))

    def advance(group_index, carried):
        leading_tap = group_index * group_length
        places = lax.dynamic_slice_in_dim(target_by_row, leading_tap, group_length, 1)
        kernels = lax.dynamic_slice_in_dim(flipped, leading_tap, group_length, 0).reshape(
            group_length * channels, channels
        )

        def accumulate(current):
            grad_rows, grad_kernel = current
            chosen = gradient_zero[places].reshape(extended_rows, group_length * channels)
            grad_rows = grad_rows + jnp.dot(chosen, kernels, preferred_element_type=jnp.float32)
            kernel_term = lax.dot_general(
                padded_features,
                chosen,
                (((0,), (0,)), ((), ())),
                preferred_element_type=jnp.float32,
            )
            kernel_term = jnp.transpose(
                kernel_term.reshape(channels, group_length, channels), (1, 0, 2)
            )
            grad_kernel = lax.dynamic_update_slice_in_dim(grad_kernel, kernel_term, leading_tap, 0)
            return (grad_rows, grad_kernel)

        return accumulate(carried)

    start = (
        jnp.zeros((extended_rows, channels), jnp.float32),
        jnp.zeros((tap_count, channels, channels), jnp.float32),
    )
    return lax.fori_loop(0, tap_count // group_length, advance, start)


def shards(features, weight, upstream, send_rows, in_rows, out_rows, tap_pair_exists):
    own_features = features[0, 0, 0]
    own_rows, channels = own_features.shape
    sends = send_rows[0, 0, 0]
    face_rows = sends.shape[1]
    source_voxels = in_rows[0, 0, 0]
    target_voxels = out_rows[0, 0, 0]
    occupancy_flags = tap_pair_exists[0, 0, 0]
    sent = own_features[sends]
    incoming = trade(sent)
    padded_features = jnp.concatenate(
        [own_features, incoming.reshape(6 * face_rows, channels)], axis=0
    )
    extended_rows = padded_features.shape[0]
    padded_zero = jnp.concatenate([padded_features, jnp.zeros((1, channels), jnp.bfloat16)], axis=0)
    forward_source, backward_target = pairing_tables(
        source_voxels, target_voxels, occupancy_flags, extended_rows
    )
    group_length, skip_dead = (9, False)
    linear_response = convolution_forward_step(padded_zero, forward_source, weight, group_length)
    sigmoid = jax.nn.sigmoid(linear_response)
    activated = (linear_response * sigmoid).astype(jnp.bfloat16)
    derivative = sigmoid * (1.0 + linear_response * (1.0 - sigmoid))
    preactivation_gradient = (upstream[0, 0, 0].astype(jnp.float32) * derivative).astype(
        jnp.bfloat16
    )
    gradient_zero = jnp.concatenate(
        [preactivation_gradient, jnp.zeros((1, channels), jnp.bfloat16)], axis=0
    )
    grad_extended, weight_partial = convolution_backward_step(
        padded_features, backward_target, weight, gradient_zero, group_length
    )
    devices_all = lax.axis_size("gx") * lax.axis_size("gy") * lax.axis_size("gz")
    scaling = float(devices_all * own_rows) ** (-0.5)
    summed = lax.psum(weight_partial, ("gx", "gy", "gz"))
    grad_weight = (summed * scaling).astype(jnp.bfloat16)
    faces_back = grad_extended[own_rows:].astype(jnp.bfloat16).reshape(6, face_rows, channels)
    returned = trade(faces_back)
    grad_features = (
        grad_extended[:own_rows]
        .at[sends.reshape(-1)]
        .add(returned.reshape(-1, channels).astype(jnp.float32))
    )
    activated = activated[None, None, None]
    grad_features = grad_features.astype(jnp.bfloat16)[None, None, None]
    return (activated, grad_features, grad_weight)


def solution(mesh):
    return jax.shard_map(
        shards,
        mesh=mesh,
        in_specs=(
            P("gx", "gy", "gz", None, None),
            P(),
            P("gx", "gy", "gz", None, None),
            P("gx", "gy", "gz", None, None),
            P("gx", "gy", "gz", None, None),
            P("gx", "gy", "gz", None, None),
            P("gx", "gy", "gz", None, None),
        ),
        out_specs=(P("gx", "gy", "gz", None, None), P("gx", "gy", "gz", None, None), P()),
        check_vma=False,
    )
```

profile of v0, /device:TPU:0, one launch (start us, length us, event | category | flops | bytes accessed | tf_op | source)
XLA Modules:
  0.0 1032.5 jit_solution(6745703560755910110)
XLA Ops:
  16.9 5.6 collective-permute-start.2
  32.9 76.2 %scatter_custom_fusion.1 = s32[20736]{0:T(1024)S(1)} fusion(s32[20736]{0:T(1024)S(1)} %reshape.225, s32[20736]{0:T(1024)S(1)} %reshape.227, s32[]{:T(128)} %constant.100.clone.1), kind=kCustom, calls=%fused_computation.70 | custom fusion | bytes 82948
  109.2 156.1 %gather_fusion.4 = s32[20736]{0:T(1024)S(1)} fusion(s32[27,768]{1,0:T(8,128)S(1)} %bitcast.88, s32[20736]{0:T(1024)S(1)} %reshape.270), kind=kCustom, calls=%fused_computation.3.clone | custom fusion | bytes 331776 | tf_op jit(solution)/shard_map/jit(take_along_axis)/gather | solution.py:41
  265.4 156.1 %gather_fusion.3 = s32[20736]{0:T(1024)S(1)} fusion(s32[27,768]{1,0:T(8,128)S(1)} %bitcast.89, s32[20736]{0:T(1024)S(1)} %reshape.270), kind=kCustom, calls=%fused_computation.clone | custom fusion | bytes 331776 | tf_op jit(solution)/shard_map/jit(take_along_axis)/gather | solution.py:40
  421.7 76.3 %scatter_custom_fusion.2 = s32[36288]{0:T(1024)S(1)} fusion(s32[20736]{0:T(1024)S(1)} %reshape.231, s32[20736]{0:T(1024)S(1)} %reshape.233, s32[]{:T(128)} %constant.102.clone.1), kind=kCustom, calls=%fused_computation.54 | custom fusion | bytes 145156
  498.1 5.7 copy.22
  511.2 100.8 %while.30 = (s32[]{:T(128)}, f32[768,256]{1,0:T(8,128)S(1)}, s32[768,27]{0,1:T(8,128)S(1)}, bf16[1345,256]{1,0:T(8,128)(2,1)S(1)}, bf16[27,256,256]{2,1,0:T(8,12...) while((s32[]{:T(128)}, f32[768,256]{1,0:T(8,128)S(1)}, s32[768,27]{0,1:T(8,128)S(1)}, ...), condition=%wide.region_2.4_spmd.clone, body=%wide.region_1.3_spmd.clone.sunk | while | flops 906390784 | bytes 23505060 | solution.py:71
  511.8 20.0 %gather_fusion = bf16[6912,256]{1,0:T(8,128)(2,1)} fusion(bf16[1345,256]{1,0:T(8,128)(2,1)S(1)} %get-tuple-element.424, s32[7168]{0:T(1024)S(1)} %pad_clamp_fusion.5), kind=kCustom, calls=%fused_computation.1.clone.clone.1 | custom fusion | bytes 7105536 | tf_op jit(solution)/shard_map/while/body/eval_jaxpr/gather | solution.py:65
  531.7 7.8 reshape.303
  545.3 20.0 %gather_fusion = bf16[6912,256]{1,0:T(8,128)(2,1)} fusion(bf16[1345,256]{1,0:T(8,128)(2,1)S(1)} %get-tuple-element.424, s32[7168]{0:T(1024)S(1)} %pad_clamp_fusion.5), kind=kCustom, calls=%fused_computation.1.clone.clone.1 | custom fusion | bytes 7105536 | tf_op jit(solution)/shard_map/while/body/eval_jaxpr/gather | solution.py:65
  565.3 7.8 reshape.303
  578.9 20.0 %gather_fusion = bf16[6912,256]{1,0:T(8,128)(2,1)} fusion(bf16[1345,256]{1,0:T(8,128)(2,1)S(1)} %get-tuple-element.424, s32[7168]{0:T(1024)S(1)} %pad_clamp_fusion.5), kind=kCustom, calls=%fused_computation.1.clone.clone.1 | custom fusion | bytes 7105536 | tf_op jit(solution)/shard_map/while/body/eval_jaxpr/gather | solution.py:65
  598.9 7.8 reshape.303
  616.8 238.7 %while.31 = (s32[]{:T(128)}, f32[1344,256]{1,0:T(8,128)}, f32[27,256,256]{2,1,0:T(8,128)}, s32[1344,27]{0,1:T(8,128)S(1)}, bf16[769,256]{1,0:T(8,128)(2,1)S(1)},...) while((s32[]{:T(128)}, f32[1344,256]{1,0:T(8,128)}, ...), condition=%wide.region_5.7_spmd.clone, body=%wide.region_4.6_spmd.clone.sunk | while | flops 3171630592 | bytes 85074704 | solution.py:111
  617.6 34.7 %gather_fusion.1 = bf16[12096,256]{1,0:T(8,128)(2,1)} fusion(bf16[769,256]{1,0:T(8,128)(2,1)S(1)} %get-tuple-element.456, s32[12288]{0:T(1024)S(1)} %pad_clamp_fusion.6), kind=kCustom, calls=%fused_computation.2.clone.clone.1 | custom fusion | bytes 12434688 | tf_op jit(solution)/shard_map/while/body/eval_jaxpr/gather | solution.py:91
  652.3 11.9 %reshape.308 = bf16[1344,2304]{1,0:T(8,128)(2,1)} reshape(bf16[12096,256]{1,0:T(8,128)(2,1)} %gather_fusion.1) | data formatting | bytes 12386304 | tf_op jit(solution)/shard_map/while/body/eval_jaxpr/reshape | solution.py:91
  664.2 6.2 fusion.51
  674.2 12.8 %reshape.307 = bf16[1344,9,256]{2,1,0:T(8,128)(2,1)} reshape(bf16[12096,256]{1,0:T(8,128)(2,1)} %gather_fusion.1) | data formatting | bytes 12386304 | tf_op jit(solution)/shard_map/while/body/eval_jaxpr/gather | solution.py:91
  686.9 8.3 fusion.50
  697.2 34.7 %gather_fusion.1 = bf16[12096,256]{1,0:T(8,128)(2,1)} fusion(bf16[769,256]{1,0:T(8,128)(2,1)S(1)} %get-tuple-element.456, s32[12288]{0:T(1024)S(1)} %pad_clamp_fusion.6), kind=kCustom, calls=%fused_computation.2.clone.clone.1 | custom fusion | bytes 12434688 | tf_op jit(solution)/shard_map/while/body/eval_jaxpr/gather | solution.py:91
  731.9 11.9 %reshape.308 = bf16[1344,2304]{1,0:T(8,128)(2,1)} reshape(bf16[12096,256]{1,0:T(8,128)(2,1)} %gather_fusion.1) | data formatting | bytes 12386304 | tf_op jit(solution)/shard_map/while/body/eval_jaxpr/reshape | solution.py:91
  743.8 6.2 fusion.51
  753.7 12.8 %reshape.307 = bf16[1344,9,256]{2,1,0:T(8,128)(2,1)} reshape(bf16[12096,256]{1,0:T(8,128)(2,1)} %gather_fusion.1) | data formatting | bytes 12386304 | tf_op jit(solution)/shard_map/while/body/eval_jaxpr/gather | solution.py:91
  766.4 8.3 fusion.50
  776.7 34.7 %gather_fusion.1 = bf16[12096,256]{1,0:T(8,128)(2,1)} fusion(bf16[769,256]{1,0:T(8,128)(2,1)S(1)} %get-tuple-element.456, s32[12288]{0:T(1024)S(1)} %pad_clamp_fusion.6), kind=kCustom, calls=%fused_computation.2.clone.clone.1 | custom fusion | bytes 12434688 | tf_op jit(solution)/shard_map/while/body/eval_jaxpr/gather | solution.py:91
  811.4 11.9 %reshape.308 = bf16[1344,2304]{1,0:T(8,128)(2,1)} reshape(bf16[12096,256]{1,0:T(8,128)(2,1)} %gather_fusion.1) | data formatting | bytes 12386304 | tf_op jit(solution)/shard_map/while/body/eval_jaxpr/reshape | solution.py:91
  823.4 6.2 fusion.51
  833.2 12.8 %reshape.307 = bf16[1344,9,256]{2,1,0:T(8,128)(2,1)} reshape(bf16[12096,256]{1,0:T(8,128)(2,1)} %gather_fusion.1) | data formatting | bytes 12386304 | tf_op jit(solution)/shard_map/while/body/eval_jaxpr/gather | solution.py:91
  845.9 8.3 fusion.50
  875.0 6.7 scatter_custom_fusion
  882.5 137.4 %all-reduce.3.cloned.1.call-done = f32[27,256,256]{2,1,0:T(8,128)} async-done(((f32[27,256,256]{2,1,0:T(8,128)}), f32[27,256,256]{2,1,0:T(8,128)}) %all-reduce.3.cloned.1.call-update) | async-done | bytes 7077904 | tf_op jit(solution)/shard_map/psum | solution.py:148
  1019.9 5.7 multiply_convert_fusion
  (147 shorter events, 86.8 us)
Async XLA Ops:
  7.2 1012.7 %all-reduce.3.cloned.1.call-start = ((), (), s32[]{:S(2)}) async-start(), calls=%async_computation | async-start | bytes 14155776 | tf_op jit(solution)/shard_map/psum | solution.py:148
  11.2 498.7 %collective-permute-start.5 = (bf16[1,96,256]{2,1,0:T(8,128)(2,1)S(1)}, bf16[1,96,256]{2,1,0:T(8,128)(2,1)S(1)}, u32[]{:S(2)}, u32[]{:S(2)}) collective-permute-start(bf16[1,96,256]{2,1,0:T(8,128)(2,1)S(1)} %get-tuple-element.321), channel_id=1, source_target_pairs={{1,0},{2,1},{3,2},{5,4},{6,5},{7,6},{9,8},{10,9},{11,10},{13,12},{... | collective-permute-start | bytes 147464 | tf_op jit(solution)/shard_map/ppermute | solution.py:17
  12.5 497.3 %collective-permute-start.4 = (bf16[1,96,256]{2,1,0:T(8,128)(2,1)S(1)}, bf16[1,96,256]{2,1,0:T(8,128)(2,1)S(1)}, u32[]{:S(2)}, u32[]{:S(2)}) collective-permute-start(bf16[1,96,256]{2,1,0:T(8,128)(2,1)S(1)} %get-tuple-element.322), channel_id=1, source_target_pairs={{0,1},{1,2},{2,3},{4,5},{5,6},{6,7},{8,9},{9,10},{10,11},{12,13},{... | collective-permute-start | bytes 147464 | tf_op jit(solution)/shard_map/ppermute | solution.py:15
  15.6 494.3 %collective-permute-start.3 = (bf16[1,96,256]{2,1,0:T(8,128)(2,1)S(1)}, bf16[1,96,256]{2,1,0:T(8,128)(2,1)S(1)}, u32[]{:S(2)}, u32[]{:S(2)}) collective-permute-start(bf16[1,96,256]{2,1,0:T(8,128)(2,1)S(1)} %get-tuple-element.323), channel_id=1, source_target_pairs={{4,0},{8,4},{12,8},{5,1},{9,5},{13,9},{6,2},{10,6},{14,10},{7,3},{... | collective-permute-start | bytes 147464 | tf_op jit(solution)/shard_map/ppermute | solution.py:17
  16.9 493.0 %collective-permute-start.2 = (bf16[1,96,256]{2,1,0:T(8,128)(2,1)S(1)}, bf16[1,96,256]{2,1,0:T(8,128)(2,1)S(1)}, u32[]{:S(2)}, u32[]{:S(2)}) collective-permute-start(bf16[1,96,256]{2,1,0:T(8,128)(2,1)S(1)} %get-tuple-element.324), channel_id=1, source_target_pairs={{0,4},{4,8},{8,12},{1,5},{5,9},{9,13},{2,6},{6,10},{10,14},{3,7},{... | collective-permute-start | bytes 147464 | tf_op jit(solution)/shard_map/ppermute | solution.py:15
  22.5 481.4 %collective-permute-start = (bf16[1,96,256]{2,1,0:T(8,128)(2,1)S(1)}, bf16[1,96,256]{2,1,0:T(8,128)(2,1)S(1)}, u32[]{:S(2)}, u32[]{:S(2)}) collective-permute-start(bf16[1,96,256]{2,1,0:T(8,128)(2,1)S(1)} %get-tuple-element.326), channel_id=1, source_target_pairs={{0,16},{1,17},{2,18},{3,19},{4,20},{5,21},{6,22},{7,23},{8,24},{9,... | collective-permute-start | bytes 147464 | tf_op jit(solution)/shard_map/ppermute | solution.py:15
  265.3 156.2 %copy-start.6 = (s32[1,1,1,27,768]{4,2,3,1,0:T(1,128)S(1)}, s32[1,1,1,27,768]{4,2,3,1,0:T(1,128)}, u32[]{:S(2)}) copy-start(s32[1,1,1,27,768]{4,2,3,1,0:T(1,128)} %param.18) | copy-start | bytes 248836
  265.4 156.2 %copy-start.7 = (s32[1,1,1,27,768]{4,2,3,1,0:T(1,128)S(1)}, s32[1,1,1,27,768]{4,2,3,1,0:T(1,128)}, u32[]{:S(2)}) copy-start(s32[1,1,1,27,768]{4,2,3,1,0:T(1,128)} %param.19) | copy-start | bytes 248836
  421.5 88.4 %copy-start = (bf16[1,1,1,768,256]{4,3,2,1,0:T(8,128)(2,1)S(1)}, bf16[1,1,1,768,256]{4,3,2,1,0:T(8,128)(2,1)}, u32[]{:S(2)}) copy-start(bf16[1,1,1,768,256]{4,3,2,1,0:T(8,128)(2,1)} %param.13) | copy-start | bytes 1179652
  503.9 6.0 collective-permute-start.1
  511.2 100.8 %copy-start.5 = (bf16[1,1,1,768,256]{4,3,2,1,0:T(8,128)(2,1)S(1)}, bf16[1,1,1,768,256]{4,3,2,1,0:T(8,128)(2,1)}, u32[]{:S(2)}) copy-start(bf16[1,1,1,768,256]{4,3,2,1,0:T(8,128)(2,1)} %param.15) | copy-start | bytes 1179652
  652.3 11.9 %copy-start.4 = (bf16[1344,256]{1,0:T(8,128)(2,1)S(1)}, bf16[1344,256]{1,0:T(8,128)(2,1)}, u32[]{:S(2)}) copy-start(bf16[1344,256]{1,0:T(8,128)(2,1)} %get-tuple-element.458) | copy-start | bytes 2064388 | tf_op jit(solution)/shard_map/while
  674.1 12.8 %copy-start.1 = (f32[1344,256]{1,0:T(8,128)S(1)}, f32[1344,256]{1,0:T(8,128)}, u32[]{:S(2)}) copy-start(f32[1344,256]{1,0:T(8,128)} %get-tuple-element.442) | copy-start | bytes 4128772 | tf_op jit(solution)/shard_map/while
  695.2 1.2 copy-start.2
  731.9 11.9 %copy-start.4 = (bf16[1344,256]{1,0:T(8,128)(2,1)S(1)}, bf16[1344,256]{1,0:T(8,128)(2,1)}, u32[]{:S(2)}) copy-start(bf16[1344,256]{1,0:T(8,128)(2,1)} %get-tuple-element.458) | copy-start | bytes 2064388 | tf_op jit(solution)/shard_map/while
  753.7 12.8 %copy-start.1 = (f32[1344,256]{1,0:T(8,128)S(1)}, f32[1344,256]{1,0:T(8,128)}, u32[]{:S(2)}) copy-start(f32[1344,256]{1,0:T(8,128)} %get-tuple-element.442) | copy-start | bytes 4128772 | tf_op jit(solution)/shard_map/while
  774.7 1.2 copy-start.2
  811.4 11.9 %copy-start.4 = (bf16[1344,256]{1,0:T(8,128)(2,1)S(1)}, bf16[1344,256]{1,0:T(8,128)(2,1)}, u32[]{:S(2)}) copy-start(bf16[1344,256]{1,0:T(8,128)(2,1)} %get-tuple-element.458) | copy-start | bytes 2064388 | tf_op jit(solution)/shard_map/while
  833.2 12.8 %copy-start.1 = (f32[1344,256]{1,0:T(8,128)S(1)}, f32[1344,256]{1,0:T(8,128)}, u32[]{:S(2)}) copy-start(f32[1344,256]{1,0:T(8,128)} %get-tuple-element.442) | copy-start | bytes 4128772 | tf_op jit(solution)/shard_map/while
  854.2 1.2 copy-start.2
  855.4 0.7 copy-start.8
  855.4 1.4 copy-start.3
  856.9 11.9 %collective-permute-start.6 = (bf16[1,96,256]{2,1,0:T(8,128)(2,1)S(1)}, bf16[1,96,256]{2,1,0:T(8,128)(2,1)S(1)}, u32[]{:S(2)}, u32[]{:S(2)}) collective-permute-start(bf16[1,96,256]{2,1,0:T(8,128)(2,1)S(1)} %get-tuple-element.320), channel_id=1, source_target_pairs={{0,16},{1,17},{2,18},{3,19},{4,20},{5,21},{6,22},{7,23},{8,24},{9,... | collective-permute-start | bytes 147464 | tf_op jit(solution)/shard_map/ppermute | solution.py:15
  858.6 16.4 %collective-permute-start.11 = (bf16[1,96,256]{2,1,0:T(8,128)(2,1)S(1)}, bf16[1,96,256]{2,1,0:T(8,128)(2,1)S(1)}, u32[]{:S(2)}, u32[]{:S(2)}) collective-permute-start(bf16[1,96,256]{2,1,0:T(8,128)(2,1)S(1)} %get-tuple-element.315), channel_id=1, source_target_pairs={{1,0},{2,1},{3,2},{5,4},{6,5},{7,6},{9,8},{10,9},{11,10},{13,12},{... | collective-permute-start | bytes 147464 | tf_op jit(solution)/shard_map/ppermute | solution.py:17
  859.9 15.1 %collective-permute-start.10 = (bf16[1,96,256]{2,1,0:T(8,128)(2,1)S(1)}, bf16[1,96,256]{2,1,0:T(8,128)(2,1)S(1)}, u32[]{:S(2)}, u32[]{:S(2)}) collective-permute-start(bf16[1,96,256]{2,1,0:T(8,128)(2,1)S(1)} %get-tuple-element.316), channel_id=1, source_target_pairs={{0,1},{1,2},{2,3},{4,5},{5,6},{6,7},{8,9},{9,10},{10,11},{12,13},{... | collective-permute-start | bytes 147464 | tf_op jit(solution)/shard_map/ppermute | solution.py:15
  862.9 12.0 %collective-permute-start.9 = (bf16[1,96,256]{2,1,0:T(8,128)(2,1)S(1)}, bf16[1,96,256]{2,1,0:T(8,128)(2,1)S(1)}, u32[]{:S(2)}, u32[]{:S(2)}) collective-permute-start(bf16[1,96,256]{2,1,0:T(8,128)(2,1)S(1)} %get-tuple-element.317), channel_id=1, source_target_pairs={{4,0},{8,4},{12,8},{5,1},{9,5},{13,9},{6,2},{10,6},{14,10},{7,3},{... | collective-permute-start | bytes 147464 | tf_op jit(solution)/shard_map/ppermute | solution.py:17
  864.2 10.7 %collective-permute-start.8 = (bf16[1,96,256]{2,1,0:T(8,128)(2,1)S(1)}, bf16[1,96,256]{2,1,0:T(8,128)(2,1)S(1)}, u32[]{:S(2)}, u32[]{:S(2)}) collective-permute-start(bf16[1,96,256]{2,1,0:T(8,128)(2,1)S(1)} %get-tuple-element.318), channel_id=1, source_target_pairs={{0,4},{4,8},{8,12},{1,5},{5,9},{9,13},{2,6},{6,10},{10,14},{3,7},{... | collective-permute-start | bytes 147464 | tf_op jit(solution)/shard_map/ppermute | solution.py:15
  868.8 6.1 collective-permute-start.7
Sparse Core Ops, SparseCore 0:
  855.6 164.2 all-reduce.2
where the time goes:
time: 1040 us; the launch traced here: 1030 us
  local copies, waits for them, and re-layouts  760 us (73%)
  waiting for transfers between devices  147 us (14%)
  matrix products  59.3 us (6%)
  starting transfers between devices  29.4 us (3%)
  other arithmetic  21.6 us (2%)
  between operations  14.6 us (1%)
    unnamed x29, local copies, waits for them, and re-layouts  161 us
    gather x3, local copies, waits for them, and re-layouts, pairing_tables(): live_at_out = jnp.take_along_axis(occupancy_flags, inverse_out, axis=1)  156 us
    gather x2, local copies, waits for them, and re-layouts, pairing_tables(): source_at_out = jnp.take_along_axis(source_voxels, inverse_out, axis=1)  156 us
    gather x6, local copies, waits for them, and re-layouts, accumulate(): gradient_zero[places].reshape(extended_rows, group_length * channels)  142 us
    psum x1, waiting for transfers between devices, shards(): summed = lax.psum(weight_partial, ('gx', 'gy', 'gz'))  137 us
    gather x6, local copies, waits for them, and re-layouts, accumulate(): gathered = padded_zero[picks].reshape(own_rows, group_length * channels)  83.2 us
    reshape x3, local copies, waits for them, and re-layouts, accumulate(): gradient_zero[places].reshape(extended_rows, group_length * channels)  35.8 us
    dot_general x3, matrix products, accumulate(): jnp.dot(chosen, kernels, preferred_element_type=jnp.float32)  24.9 us
  transfers between devices with their start and end apart: 13, of which 3 were waited for; matrix products, arithmetic and copies ran while one was open for 47% of the time, Pallas kernels for 0%

commit v1 on v0

--- a/solution.py
+++ b/solution.py
@@ -145,7 +145,7 @@
     )
     devices_all = lax.axis_size("gx") * lax.axis_size("gy") * lax.axis_size("gz")
     scaling = float(devices_all * own_rows) ** (-0.5)
-    summed = lax.psum(weight_partial, ("gx", "gy", "gz"))
+    summed = lax.psum(lax.psum(weight_partial, ("gy", "gz")), "gx")
     grad_weight = (summed * scaling).astype(jnp.bfloat16)
     faces_back = grad_extended[own_rows:].astype(jnp.bfloat16).reshape(6, face_rows, channels)
     returned = trade(faces_back)

time: 1040 us -> 1190 us (1.14)
  waiting for transfers between devices: 147 us -> 305 us
    psum x1 -> x2, waiting for transfers between devices: 137 us -> 295 us  [shards(): summed = lax.psum(lax.psum(weight_partial, ('gy', 'gz')), 'gx')]
  transfers between devices with their start and end apart: 13 -> 14, of which waited for: 3 -> 4; matrix products, arithmetic and copies ran while one was open for 47% -> 41% of each run, Pallas kernels for 0% -> 0%
where the time goes in v1:
time: 1190 us
  local copies, waits for them, and re-layouts  759 us (64%)
  waiting for transfers between devices  305 us (26%)
  matrix products  59.3 us (5%)
  starting transfers between devices  31.2 us (3%)
  other arithmetic  21.6 us (2%)
  between operations  14.6 us (1%)
    psum x2, waiting for transfers between devices, shards(): summed = lax.psum(lax.psum(weight_partial, ('gy', 'gz')), 'gx')  295 us
    unnamed x29, local copies, waits for them, and re-layouts  160 us
    gather x3, local copies, waits for them, and re-layouts, pairing_tables(): live_at_out = jnp.take_along_axis(occupancy_flags, inverse_out, axis=1)  156 us
    gather x2, local copies, waits for them, and re-layouts, pairing_tables(): source_at_out = jnp.take_along_axis(source_voxels, inverse_out, axis=1)  156 us
    gather x6, local copies, waits for them, and re-layouts, accumulate(): gradient_zero[places].reshape(extended_rows, group_length * channels)  142 us
    gather x6, local copies, waits for them, and re-layouts, accumulate(): gathered = padded_zero[picks].reshape(own_rows, group_length * channels)  83.2 us
    reshape x3, local copies, waits for them, and re-layouts, accumulate(): gradient_zero[places].reshape(extended_rows, group_length * channels)  35.8 us
    dot_general x3, matrix products, accumulate(): jnp.dot(chosen, kernels, preferred_element_type=jnp.float32)  24.9 us
  transfers between devices with their start and end apart: 14, of which 4 were waited for; matrix products, arithmetic and copies ran while one was open for 41% of the time, Pallas kernels for 0%

profile of v1, /device:TPU:0, one launch (start us, length us, event | category | flops | bytes accessed | tf_op | source)
XLA Modules:
  0.0 1191.6 jit_solution(16034327733969883778)
XLA Ops:
  32.9 76.2 %scatter_custom_fusion.1 = s32[20736]{0:T(1024)S(1)} fusion(s32[20736]{0:T(1024)S(1)} %reshape.225, s32[20736]{0:T(1024)S(1)} %reshape.227, s32[]{:T(128)} %constant.100.clone.1), kind=kCustom, calls=%fused_computation.70 | custom fusion | bytes 82948
  109.2 156.1 %gather_fusion.4 = s32[20736]{0:T(1024)S(1)} fusion(s32[27,768]{1,0:T(8,128)S(1)} %bitcast.88, s32[20736]{0:T(1024)S(1)} %reshape.270), kind=kCustom, calls=%fused_computation.3.clone | custom fusion | bytes 331776 | tf_op jit(solution)/shard_map/jit(take_along_axis)/gather | solution.py:41
  265.4 156.1 %gather_fusion.3 = s32[20736]{0:T(1024)S(1)} fusion(s32[27,768]{1,0:T(8,128)S(1)} %bitcast.89, s32[20736]{0:T(1024)S(1)} %reshape.270), kind=kCustom, calls=%fused_computation.clone | custom fusion | bytes 331776 | tf_op jit(solution)/shard_map/jit(take_along_axis)/gather | solution.py:40
  421.7 76.3 %scatter_custom_fusion.2 = s32[36288]{0:T(1024)S(1)} fusion(s32[20736]{0:T(1024)S(1)} %reshape.231, s32[20736]{0:T(1024)S(1)} %reshape.233, s32[]{:T(128)} %constant.102.clone.1), kind=kCustom, calls=%fused_computation.54 | custom fusion | bytes 145156
  511.2 100.8 %while.30 = (s32[]{:T(128)}, f32[768,256]{1,0:T(8,128)S(1)}, s32[768,27]{0,1:T(8,128)S(1)}, bf16[1345,256]{1,0:T(8,128)(2,1)S(1)}, bf16[27,256,256]{2,1,0:T(8,12...) while((s32[]{:T(128)}, f32[768,256]{1,0:T(8,128)S(1)}, s32[768,27]{0,1:T(8,128)S(1)}, ...), condition=%wide.region_2.4_spmd.clone, body=%wide.region_1.3_spmd.clone.sunk | while | flops 906390784 | bytes 23505060 | solution.py:71
  511.8 20.0 %gather_fusion = bf16[6912,256]{1,0:T(8,128)(2,1)} fusion(bf16[1345,256]{1,0:T(8,128)(2,1)S(1)} %get-tuple-element.424, s32[7168]{0:T(1024)S(1)} %pad_clamp_fusion.5), kind=kCustom, calls=%fused_computation.1.clone.clone.1 | custom fusion | bytes 7105536 | tf_op jit(solution)/shard_map/while/body/eval_jaxpr/gather | solution.py:65
  531.7 7.8 reshape.303
  545.3 20.0 %gather_fusion = bf16[6912,256]{1,0:T(8,128)(2,1)} fusion(bf16[1345,256]{1,0:T(8,128)(2,1)S(1)} %get-tuple-element.424, s32[7168]{0:T(1024)S(1)} %pad_clamp_fusion.5), kind=kCustom, calls=%fused_computation.1.clone.clone.1 | custom fusion | bytes 7105536 | tf_op jit(solution)/shard_map/while/body/eval_jaxpr/gather | solution.py:65
  565.3 7.8 reshape.303
  578.9 20.0 %gather_fusion = bf16[6912,256]{1,0:T(8,128)(2,1)} fusion(bf16[1345,256]{1,0:T(8,128)(2,1)S(1)} %get-tuple-element.424, s32[7168]{0:T(1024)S(1)} %pad_clamp_fusion.5), kind=kCustom, calls=%fused_computation.1.clone.clone.1 | custom fusion | bytes 7105536 | tf_op jit(solution)/shard_map/while/body/eval_jaxpr/gather | solution.py:65
  598.9 7.8 reshape.303
  616.8 238.7 %while.31 = (s32[]{:T(128)}, f32[1344,256]{1,0:T(8,128)}, f32[27,256,256]{2,1,0:T(8,128)}, s32[1344,27]{0,1:T(8,128)S(1)}, bf16[769,256]{1,0:T(8,128)(2,1)S(1)},...) while((s32[]{:T(128)}, f32[1344,256]{1,0:T(8,128)}, ...), condition=%wide.region_5.7_spmd.clone, body=%wide.region_4.6_spmd.clone.sunk | while | flops 3171630592 | bytes 85074704 | solution.py:111
  617.6 34.7 %gather_fusion.1 = bf16[12096,256]{1,0:T(8,128)(2,1)} fusion(bf16[769,256]{1,0:T(8,128)(2,1)S(1)} %get-tuple-element.456, s32[12288]{0:T(1024)S(1)} %pad_clamp_fusion.6), kind=kCustom, calls=%fused_computation.2.clone.clone.1 | custom fusion | bytes 12434688 | tf_op jit(solution)/shard_map/while/body/eval_jaxpr/gather | solution.py:91
  652.3 11.9 %reshape.308 = bf16[1344,2304]{1,0:T(8,128)(2,1)} reshape(bf16[12096,256]{1,0:T(8,128)(2,1)} %gather_fusion.1) | data formatting | bytes 12386304 | tf_op jit(solution)/shard_map/while/body/eval_jaxpr/reshape | solution.py:91
  664.2 6.2 fusion.51
  674.2 12.8 %reshape.307 = bf16[1344,9,256]{2,1,0:T(8,128)(2,1)} reshape(bf16[12096,256]{1,0:T(8,128)(2,1)} %gather_fusion.1) | data formatting | bytes 12386304 | tf_op jit(solution)/shard_map/while/body/eval_jaxpr/gather | solution.py:91
  686.9 8.3 fusion.50
  697.2 34.7 %gather_fusion.1 = bf16[12096,256]{1,0:T(8,128)(2,1)} fusion(bf16[769,256]{1,0:T(8,128)(2,1)S(1)} %get-tuple-element.456, s32[12288]{0:T(1024)S(1)} %pad_clamp_fusion.6), kind=kCustom, calls=%fused_computation.2.clone.clone.1 | custom fusion | bytes 12434688 | tf_op jit(solution)/shard_map/while/body/eval_jaxpr/gather | solution.py:91
  731.9 11.9 %reshape.308 = bf16[1344,2304]{1,0:T(8,128)(2,1)} reshape(bf16[12096,256]{1,0:T(8,128)(2,1)} %gather_fusion.1) | data formatting | bytes 12386304 | tf_op jit(solution)/shard_map/while/body/eval_jaxpr/reshape | solution.py:91
  743.8 6.2 fusion.51
  753.7 12.8 %reshape.307 = bf16[1344,9,256]{2,1,0:T(8,128)(2,1)} reshape(bf16[12096,256]{1,0:T(8,128)(2,1)} %gather_fusion.1) | data formatting | bytes 12386304 | tf_op jit(solution)/shard_map/while/body/eval_jaxpr/gather | solution.py:91
  766.4 8.3 fusion.50
  776.7 34.7 %gather_fusion.1 = bf16[12096,256]{1,0:T(8,128)(2,1)} fusion(bf16[769,256]{1,0:T(8,128)(2,1)S(1)} %get-tuple-element.456, s32[12288]{0:T(1024)S(1)} %pad_clamp_fusion.6), kind=kCustom, calls=%fused_computation.2.clone.clone.1 | custom fusion | bytes 12434688 | tf_op jit(solution)/shard_map/while/body/eval_jaxpr/gather | solution.py:91
  811.4 11.9 %reshape.308 = bf16[1344,2304]{1,0:T(8,128)(2,1)} reshape(bf16[12096,256]{1,0:T(8,128)(2,1)} %gather_fusion.1) | data formatting | bytes 12386304 | tf_op jit(solution)/shard_map/while/body/eval_jaxpr/reshape | solution.py:91
  823.4 6.2 fusion.51
  833.2 12.8 %reshape.307 = bf16[1344,9,256]{2,1,0:T(8,128)(2,1)} reshape(bf16[12096,256]{1,0:T(8,128)(2,1)} %gather_fusion.1) | data formatting | bytes 12386304 | tf_op jit(solution)/shard_map/while/body/eval_jaxpr/gather | solution.py:91
  845.9 8.3 fusion.50
  855.5 149.8 %all-reduce.4.cloned.1.call-done = f32[27,256,256]{2,1,0:T(8,128)} async-done(((f32[27,256,256]{2,1,0:T(8,128)}), f32[27,256,256]{2,1,0:T(8,128)}) %all-reduce.4.cloned.1.call-update) | async-done | bytes 7077904 | tf_op jit(solution)/shard_map/psum | solution.py:148
  1020.5 6.1 collective-permute-done.7
  1026.7 6.7 scatter_custom_fusion
  1034.2 144.8 %all-reduce.6.cloned.1.call-done = f32[27,256,256]{2,1,0:T(8,128)} async-done(((f32[27,256,256]{2,1,0:T(8,128)}), f32[27,256,256]{2,1,0:T(8,128)}) %all-reduce.6.cloned.1.call-update) | async-done | bytes 7077904 | tf_op jit(solution)/shard_map/psum | solution.py:148
  1179.1 5.7 multiply_convert_fusion
  (150 shorter events, 93.9 us)
Async XLA Ops:
  7.2 998.1 %all-reduce.4.cloned.1.call-start = ((), (), s32[]{:S(2)}) async-start(), calls=%async_computation | async-start | bytes 14155776 | tf_op jit(solution)/shard_map/psum | solution.py:148
  11.2 498.7 %collective-permute-start.5 = (bf16[1,96,256]{2,1,0:T(8,128)(2,1)S(1)}, bf16[1,96,256]{2,1,0:T(8,128)(2,1)S(1)}, u32[]{:S(2)}, u32[]{:S(2)}) collective-permute-start(bf16[1,96,256]{2,1,0:T(8,128)(2,1)S(1)} %get-tuple-element.321), channel_id=1, source_target_pairs={{1,0},{2,1},{3,2},{5,4},{6,5},{7,6},{9,8},{10,9},{11,10},{13,12},{... | collective-permute-start | bytes 147464 | tf_op jit(solution)/shard_map/ppermute | solution.py:17
  12.5 497.3 %collective-permute-start.4 = (bf16[1,96,256]{2,1,0:T(8,128)(2,1)S(1)}, bf16[1,96,256]{2,1,0:T(8,128)(2,1)S(1)}, u32[]{:S(2)}, u32[]{:S(2)}) collective-permute-start(bf16[1,96,256]{2,1,0:T(8,128)(2,1)S(1)} %get-tuple-element.322), channel_id=1, source_target_pairs={{0,1},{1,2},{2,3},{4,5},{5,6},{6,7},{8,9},{9,10},{10,11},{12,13},{... | collective-permute-start | bytes 147464 | tf_op jit(solution)/shard_map/ppermute | solution.py:15
  15.6 494.3 %collective-permute-start.3 = (bf16[1,96,256]{2,1,0:T(8,128)(2,1)S(1)}, bf16[1,96,256]{2,1,0:T(8,128)(2,1)S(1)}, u32[]{:S(2)}, u32[]{:S(2)}) collective-permute-start(bf16[1,96,256]{2,1,0:T(8,128)(2,1)S(1)} %get-tuple-element.323), channel_id=1, source_target_pairs={{4,0},{8,4},{12,8},{5,1},{9,5},{13,9},{6,2},{10,6},{14,10},{7,3},{... | collective-permute-start | bytes 147464 | tf_op jit(solution)/shard_map/ppermute | solution.py:17
  16.9 493.0 %collective-permute-start.2 = (bf16[1,96,256]{2,1,0:T(8,128)(2,1)S(1)}, bf16[1,96,256]{2,1,0:T(8,128)(2,1)S(1)}, u32[]{:S(2)}, u32[]{:S(2)}) collective-permute-start(bf16[1,96,256]{2,1,0:T(8,128)(2,1)S(1)} %get-tuple-element.324), channel_id=1, source_target_pairs={{0,4},{4,8},{8,12},{1,5},{5,9},{9,13},{2,6},{6,10},{10,14},{3,7},{... | collective-permute-start | bytes 147464 | tf_op jit(solution)/shard_map/ppermute | solution.py:15
  22.5 481.4 %collective-permute-start = (bf16[1,96,256]{2,1,0:T(8,128)(2,1)S(1)}, bf16[1,96,256]{2,1,0:T(8,128)(2,1)S(1)}, u32[]{:S(2)}, u32[]{:S(2)}) collective-permute-start(bf16[1,96,256]{2,1,0:T(8,128)(2,1)S(1)} %get-tuple-element.326), channel_id=1, source_target_pairs={{0,16},{1,17},{2,18},{3,19},{4,20},{5,21},{6,22},{7,23},{8,24},{9,... | collective-permute-start | bytes 147464 | tf_op jit(solution)/shard_map/ppermute | solution.py:15
  265.3 156.2 %copy-start.6 = (s32[1,1,1,27,768]{4,2,3,1,0:T(1,128)S(1)}, s32[1,1,1,27,768]{4,2,3,1,0:T(1,128)}, u32[]{:S(2)}) copy-start(s32[1,1,1,27,768]{4,2,3,1,0:T(1,128)} %param.18) | copy-start | bytes 248836
  265.4 156.2 %copy-start.7 = (s32[1,1,1,27,768]{4,2,3,1,0:T(1,128)S(1)}, s32[1,1,1,27,768]{4,2,3,1,0:T(1,128)}, u32[]{:S(2)}) copy-start(s32[1,1,1,27,768]{4,2,3,1,0:T(1,128)} %param.19) | copy-start | bytes 248836
  421.5 88.4 %copy-start = (bf16[1,1,1,768,256]{4,3,2,1,0:T(8,128)(2,1)S(1)}, bf16[1,1,1,768,256]{4,3,2,1,0:T(8,128)(2,1)}, u32[]{:S(2)}) copy-start(bf16[1,1,1,768,256]{4,3,2,1,0:T(8,128)(2,1)} %param.13) | copy-start | bytes 1179652
  503.9 6.0 collective-permute-start.1
  511.2 100.8 %copy-start.5 = (bf16[1,1,1,768,256]{4,3,2,1,0:T(8,128)(2,1)S(1)}, bf16[1,1,1,768,256]{4,3,2,1,0:T(8,128)(2,1)}, u32[]{:S(2)}) copy-start(bf16[1,1,1,768,256]{4,3,2,1,0:T(8,128)(2,1)} %param.15) | copy-start | bytes 1179652
  652.3 11.9 %copy-start.4 = (bf16[1344,256]{1,0:T(8,128)(2,1)S(1)}, bf16[1344,256]{1,0:T(8,128)(2,1)}, u32[]{:S(2)}) copy-start(bf16[1344,256]{1,0:T(8,128)(2,1)} %get-tuple-element.458) | copy-start | bytes 2064388 | tf_op jit(solution)/shard_map/while
  674.1 12.8 %copy-start.1 = (f32[1344,256]{1,0:T(8,128)S(1)}, f32[1344,256]{1,0:T(8,128)}, u32[]{:S(2)}) copy-start(f32[1344,256]{1,0:T(8,128)} %get-tuple-element.442) | copy-start | bytes 4128772 | tf_op jit(solution)/shard_map/while
  695.2 1.2 copy-start.2
  731.9 11.9 %copy-start.4 = (bf16[1344,256]{1,0:T(8,128)(2,1)S(1)}, bf16[1344,256]{1,0:T(8,128)(2,1)}, u32[]{:S(2)}) copy-start(bf16[1344,256]{1,0:T(8,128)(2,1)} %get-tuple-element.458) | copy-start | bytes 2064388 | tf_op jit(solution)/shard_map/while
  753.7 12.8 %copy-start.1 = (f32[1344,256]{1,0:T(8,128)S(1)}, f32[1344,256]{1,0:T(8,128)}, u32[]{:S(2)}) copy-start(f32[1344,256]{1,0:T(8,128)} %get-tuple-element.442) | copy-start | bytes 4128772 | tf_op jit(solution)/shard_map/while
  774.7 1.2 copy-start.2
  811.4 11.9 %copy-start.4 = (bf16[1344,256]{1,0:T(8,128)(2,1)S(1)}, bf16[1344,256]{1,0:T(8,128)(2,1)}, u32[]{:S(2)}) copy-start(bf16[1344,256]{1,0:T(8,128)(2,1)} %get-tuple-element.458) | copy-start | bytes 2064388 | tf_op jit(solution)/shard_map/while
  833.2 12.8 %copy-start.1 = (f32[1344,256]{1,0:T(8,128)S(1)}, f32[1344,256]{1,0:T(8,128)}, u32[]{:S(2)}) copy-start(f32[1344,256]{1,0:T(8,128)} %get-tuple-element.442) | copy-start | bytes 4128772 | tf_op jit(solution)/shard_map/while
  854.2 1.2 copy-start.2
  855.4 149.9 %copy-start.8 = (s32[1,1,1,6,96]{4,2,3,1,0:T(1,128)S(1)}, s32[1,1,1,6,96]{4,2,3,1,0:T(1,128)}, u32[]{:S(2)}) copy-start(s32[1,1,1,6,96]{4,2,3,1,0:T(1,128)} %param.16) | copy-start | bytes 6916
  855.4 150.0 %copy-start.3 = (f32[1344,256]{1,0:T(8,128)S(1)}, f32[1344,256]{1,0:T(8,128)}, u32[]{:S(2)}) copy-start(f32[1344,256]{1,0:T(8,128)} %get-tuple-element.224) | copy-start | bytes 4128772
  855.5 323.6 %all-reduce.6.cloned.1.call-start = ((), (), s32[]{:S(2)}) async-start(), calls=%async_computation.1 | async-start | bytes 14155776 | tf_op jit(solution)/shard_map/psum | solution.py:148
  1005.5 13.7 %collective-permute-start.6 = (bf16[1,96,256]{2,1,0:T(8,128)(2,1)S(1)}, bf16[1,96,256]{2,1,0:T(8,128)(2,1)S(1)}, u32[]{:S(2)}, u32[]{:S(2)}) collective-permute-start(bf16[1,96,256]{2,1,0:T(8,128)(2,1)S(1)} %get-tuple-element.320), channel_id=1, source_target_pairs={{0,16},{1,17},{2,18},{3,19},{4,20},{5,21},{6,22},{7,23},{8,24},{9,... | collective-permute-start | bytes 147464 | tf_op jit(solution)/shard_map/ppermute | solution.py:15
  1009.0 17.7 %collective-permute-start.11 = (bf16[1,96,256]{2,1,0:T(8,128)(2,1)S(1)}, bf16[1,96,256]{2,1,0:T(8,128)(2,1)S(1)}, u32[]{:S(2)}, u32[]{:S(2)}) collective-permute-start(bf16[1,96,256]{2,1,0:T(8,128)(2,1)S(1)} %get-tuple-element.315), channel_id=1, source_target_pairs={{1,0},{2,1},{3,2},{5,4},{6,5},{7,6},{9,8},{10,9},{11,10},{13,12},{... | collective-permute-start | bytes 147464 | tf_op jit(solution)/shard_map/ppermute | solution.py:17
  1010.3 16.3 %collective-permute-start.10 = (bf16[1,96,256]{2,1,0:T(8,128)(2,1)S(1)}, bf16[1,96,256]{2,1,0:T(8,128)(2,1)S(1)}, u32[]{:S(2)}, u32[]{:S(2)}) collective-permute-start(bf16[1,96,256]{2,1,0:T(8,128)(2,1)S(1)} %get-tuple-element.316), channel_id=1, source_target_pairs={{0,1},{1,2},{2,3},{4,5},{5,6},{6,7},{8,9},{9,10},{10,11},{12,13},{... | collective-permute-start | bytes 147464 | tf_op jit(solution)/shard_map/ppermute | solution.py:15
  1013.4 13.3 %collective-permute-start.9 = (bf16[1,96,256]{2,1,0:T(8,128)(2,1)S(1)}, bf16[1,96,256]{2,1,0:T(8,128)(2,1)S(1)}, u32[]{:S(2)}, u32[]{:S(2)}) collective-permute-start(bf16[1,96,256]{2,1,0:T(8,128)(2,1)S(1)} %get-tuple-element.317), channel_id=1, source_target_pairs={{4,0},{8,4},{12,8},{5,1},{9,5},{13,9},{6,2},{10,6},{14,10},{7,3},{... | collective-permute-start | bytes 147464 | tf_op jit(solution)/shard_map/ppermute | solution.py:17
  1014.7 12.0 %collective-permute-start.8 = (bf16[1,96,256]{2,1,0:T(8,128)(2,1)S(1)}, bf16[1,96,256]{2,1,0:T(8,128)(2,1)S(1)}, u32[]{:S(2)}, u32[]{:S(2)}) collective-permute-start(bf16[1,96,256]{2,1,0:T(8,128)(2,1)S(1)} %get-tuple-element.318), channel_id=1, source_target_pairs={{0,4},{4,8},{8,12},{1,5},{5,9},{9,13},{2,6},{6,10},{10,14},{3,7},{... | collective-permute-start | bytes 147464 | tf_op jit(solution)/shard_map/ppermute | solution.py:15
  1019.2 7.4 collective-permute-start.7
Sparse Core Ops, SparseCore 0:
  855.6 149.6 all-reduce.3
  1007.7 171.2 all-reduce.5
